TPU v7x, 32 devices: a whole 2x2x4 slice. The times are simulated.
32 devices in a mesh: samp: 8 (over z, x), state: 4 (over y, core).
Axes of the slice: x: 2, y: 2, z: 4, core: 2. Of those that a mesh axis runs over, the one named last changes fastest.
Arguments:
- energies: bfloat16 [4096, 131072], P('state', 'samp'), may hold values from -12 to 12
- offsets: float32 [4096, 1024], P('state', 'samp'), may hold values from -250 to 250
- counts: int32 [4096], P('state'), may hold values from 1 to 31745, as said below
- labels: int32 [131072], P('samp'), may hold values from 0 to 4095
Outputs:
- free_energy: float32 [4096], P('state')
- own_log_probability: float32 [131072], P('samp')
Inputs may be any that keep to these rules, and one draw needn't show every extreme that they name: counts[k] is the number of samples n with labels[n] = k; every state has a sample, state 4096 - 1 has exactly one, and state 0 has the most.
All inputs are finite; a program needn't handle non-finite values.
Results may differ from a plain program's by a relative error of at most 0.0003.
Values sent between devices are 32-bit elements; how exact they have to be, the bound alone decides.
A program may use at most 256 MiB of HBM per device.

v0:
```python
import jax
import jax.numpy as jnp
from jax import lax
from jax.sharding import PartitionSpec as P

ITERS = 3


def from_root(value, axis, root):
    mine = lax.axis_index(axis) == root
    return lax.psum(jnp.where(mine, value, jnp.zeros_like(value)), axis)


def local_energy(energies, offsets):
    rows, width = energies.shape
    nblk = offsets.shape[1]
    shaped = energies.astype(jnp.float32).reshape(rows, nblk, width // nblk)
    return (shaped + offsets[:, :, None]).reshape(rows, width)


def sample_denominator(energies, offsets, lead):
    terms = lead[:, None] - local_energy(energies, offsets)
    width = terms.shape[1]
    best = jnp.max(terms, axis=0)
    total = jnp.sum(jnp.exp(terms - best[None, :]), axis=0)
    groups = lax.axis_size("state")
    parts = (
        lax.all_to_all(
            best.reshape(groups, width // groups), "state", split_axis=0, concat_axis=0, tiled=True
        ),
        lax.all_to_all(
            total.reshape(groups, width // groups), "state", split_axis=0, concat_axis=0, tiled=True
        ),
    )
    peak = jnp.max(parts[0], axis=0)
    whole = jnp.sum(parts[1] * jnp.exp(parts[0] - peak[None, :]), axis=0)
    return lax.all_gather(peak + jnp.log(whole), "state", axis=0, tiled=True)


def state_update(energies, offsets, denom):
    terms = -local_energy(energies, offsets) - denom[None, :]
    best = lax.pmax(jnp.max(terms, axis=1), "samp")
    total = lax.psum(jnp.sum(jnp.exp(terms - best[:, None]), axis=1), "samp")
    return -(best + jnp.log(total))


def own_terms_local(energies, offsets, lead, local_label):
    rows, width = energies.shape
    nblk = offsets.shape[1]
    block_size = width // nblk
    span = min(width, max(block_size, 512))
    span = span - span % block_size
    while width % span != 0:
        span = span - block_size
    steps_count = width // span
    row_ids = jnp.arange(rows, dtype=jnp.int32)

    def one(index):
        start = index * span
        part = lax.dynamic_slice_in_dim(energies, start, span, 1).astype(jnp.float32)
        shift = lax.dynamic_slice_in_dim(
            offsets, index * (span // block_size), span // block_size, 1
        )
        energy_part = (
            part.reshape(rows, span // block_size, block_size) + shift[:, :, None]
        ).reshape(rows, span)
        wanted = lax.dynamic_slice_in_dim(local_label, start, span, 0)
        match = row_ids[:, None] == wanted[None, :]
        return jnp.sum(jnp.where(match, lead[:, None] - energy_part, 0.0), axis=0)

    return lax.map(one, jnp.arange(steps_count, dtype=jnp.int32)).reshape(width)


def shards(energies, offsets, counts, labels):
    rows, width = energies.shape
    logc = jnp.log(counts.astype(jnp.float32))
    free = jnp.zeros((rows,), jnp.float32)
    for step in range(ITERS):
        denom = sample_denominator(energies, offsets, logc + free)
        free = state_update(energies, offsets, denom)
    lead = logc + free
    denom = sample_denominator(energies, offsets, lead)
    local_label = labels - lax.axis_index("state") * rows
    picked = own_terms_local(energies, offsets, lead, local_label)
    own = lax.psum(picked, "state") - denom
    anchor_value = from_root(free[0:1], "state", 0)
    return (free - anchor_value[0], own)


def solution(mesh):
    return jax.shard_map(
        shards,
        mesh=mesh,
        in_specs=(P("state", "samp"), P("state", "samp"), P("state"), P("samp")),
        out_specs=(P("state"), P("samp")),
        check_vma=False,
    )
```

profile of v0, /device:TPU:0, one launch (start us, length us, event | category | flops | bytes accessed | tf_op | source)
XLA Modules:
  0.0 765.3 jit_solution(17431815662996339874)
XLA Ops:
  7.9 22.2 %add.48 = f32[1024,128,128]{2,1,0:T(8,128)} broadcast(f32[1024,128]{1,0:T(8,128)} %param.7), dimensions={0,1} | broadcast | bytes 67633152 | tf_op jit(solution)/shard_map/add | solution.py:18
  30.0 74.5 %subtract_reduce_fusion.6 = (f32[16384]{0:T(1024)}, f32[1024,16384]{1,0:T(8,128)}) fusion(f32[1024]{0:T(1024)S(1)} %convert_log_fusion, f32[128,8,128,128]{3,2,1,0:T(8,128)} %bitcast.23, bf16[1024,16384]{1,0:T(8,128)(2,1)} %param.6), kind=kLoop, calls=%fused_computation.21 | loop fusion | flops 67092480 | bytes 167841792 | tf_op jit(solution)/shard_map/reduce_max | solution.py:24
  108.8 24.4 %exponential_reduce_fusion.6 = f32[16384]{0:T(1024)} fusion(f32[1024,16384]{1,0:T(8,128)} %get-tuple-element.78, f32[16384]{0:T(1024)} %get-tuple-element.77, f32[1024]{0:T(1024)S(1)} %convert_log_fusion), kind=kLoop, calls=%fused_computation.14 | loop fusion | flops 50315264 | bytes 67244032 | tf_op jit(solution)/shard_map/reduce_sum | solution.py:25
  146.0 21.0 %subtract_reduce_fusion.5 = f32[1024]{0:T(1024)S(1)} fusion(f32[1024,16384]{1,0:T(8,128)} %get-tuple-element.78, f32[16384]{0:T(1024)S(1)} %all_gather.12), kind=kLoop, calls=%fused_computation.20 | loop fusion | flops 50330624 | bytes 67178496 | tf_op jit(solution)/shard_map/reduce_max | solution.py:42
  167.0 22.1 %pmax.21 = f32[1024]{0:T(1024)S(1)} all-reduce(f32[1024]{0:T(1024)S(1)} %subtract_reduce_fusion.5), channel_id=1, replica_groups=mesh['samp'=8,'state'=4] {'samp'}, use_global_device_ids=true, to_apply=%region_5.0 | all-reduce | flops 1024 | bytes 8192 | tf_op jit(solution)/shard_map/pmax | solution.py:42
  189.1 21.4 %exponential_reduce_fusion.5 = f32[1024]{0:T(1024)S(1)} fusion(f32[1024,16384]{1,0:T(8,128)} %get-tuple-element.78, f32[1024]{0:T(1024)S(1)} %pmax.21, f32[16384]{0:T(1024)S(1)} %all_gather.12), kind=kLoop, calls=%fused_computation.13 | loop fusion | flops 67107840 | bytes 67182592 | tf_op jit(solution)/shard_map/reduce_sum | solution.py:43
  210.5 17.1 %psum.35 = f32[1024]{0:T(1024)S(1)} all-reduce(f32[1024]{0:T(1024)S(1)} %exponential_reduce_fusion.5), channel_id=1, replica_groups=mesh['samp'=8,'state'=4] {'samp'}, use_global_device_ids=true, to_apply=%region_7.0 | all-reduce | flops 1024 | bytes 8192 | tf_op jit(solution)/shard_map/psum | solution.py:43
  227.7 21.5 %subtract_reduce_fusion.4 = f32[16384]{0:T(1024)} fusion(f32[1024,16384]{1,0:T(8,128)} %get-tuple-element.78, f32[1024]{0:T(1024)S(1)} %negate_add_fusion.1), kind=kLoop, calls=%fused_computation.19 | loop fusion | flops 33538048 | bytes 67178496 | tf_op jit(solution)/shard_map/reduce_max | solution.py:24
  252.4 24.4 %exponential_reduce_fusion.4 = f32[16384]{0:T(1024)} fusion(f32[1024,16384]{1,0:T(8,128)} %get-tuple-element.78, f32[16384]{0:T(1024)} %subtract_reduce_fusion.4, f32[1024]{0:T(1024)S(1)} %negate_add_fusion.1), kind=kLoop, calls=%fused_computation.12 | loop fusion | flops 50315264 | bytes 67244032 | tf_op jit(solution)/shard_map/reduce_sum | solution.py:25
  289.6 21.0 %subtract_reduce_fusion.3 = f32[1024]{0:T(1024)S(1)} fusion(f32[1024,16384]{1,0:T(8,128)} %get-tuple-element.78, f32[16384]{0:T(1024)S(1)} %all_gather.13), kind=kLoop, calls=%fused_computation.18 | loop fusion | flops 50330624 | bytes 67178496 | tf_op jit(solution)/shard_map/reduce_max | solution.py:42
  310.7 19.3 %pmax.22 = f32[1024]{0:T(1024)S(1)} all-reduce(f32[1024]{0:T(1024)S(1)} %subtract_reduce_fusion.3), channel_id=1, replica_groups=mesh['samp'=8,'state'=4] {'samp'}, use_global_device_ids=true, to_apply=%region_13.0 | all-reduce | flops 1024 | bytes 8192 | tf_op jit(solution)/shard_map/pmax | solution.py:42
  330.0 21.4 %exponential_reduce_fusion.3 = f32[1024]{0:T(1024)S(1)} fusion(f32[1024,16384]{1,0:T(8,128)} %get-tuple-element.78, f32[1024]{0:T(1024)S(1)} %pmax.22, f32[16384]{0:T(1024)S(1)} %all_gather.13), kind=kLoop, calls=%fused_computation.11 | loop fusion | flops 67107840 | bytes 67182592 | tf_op jit(solution)/shard_map/reduce_sum | solution.py:43
  351.3 17.1 %psum.36 = f32[1024]{0:T(1024)S(1)} all-reduce(f32[1024]{0:T(1024)S(1)} %exponential_reduce_fusion.3), channel_id=1, replica_groups=mesh['samp'=8,'state'=4] {'samp'}, use_global_device_ids=true, to_apply=%region_15.0 | all-reduce | flops 1024 | bytes 8192 | tf_op jit(solution)/shard_map/psum | solution.py:43
  368.5 21.5 %subtract_reduce_fusion.2 = f32[16384]{0:T(1024)} fusion(f32[1024,16384]{1,0:T(8,128)} %get-tuple-element.78, f32[1024]{0:T(1024)S(1)} %negate_add_fusion), kind=kLoop, calls=%fused_computation.17 | loop fusion | flops 33538048 | bytes 67178496 | tf_op jit(solution)/shard_map/reduce_max | solution.py:24
  393.3 24.4 %exponential_reduce_fusion.2 = f32[16384]{0:T(1024)} fusion(f32[1024,16384]{1,0:T(8,128)} %get-tuple-element.78, f32[16384]{0:T(1024)} %subtract_reduce_fusion.2, f32[1024]{0:T(1024)S(1)} %negate_add_fusion), kind=kLoop, calls=%fused_computation.10 | loop fusion | flops 50315264 | bytes 67244032 | tf_op jit(solution)/shard_map/reduce_sum | solution.py:25
  430.5 21.0 %subtract_reduce_fusion.1 = f32[1024]{0:T(1024)S(1)} fusion(f32[1024,16384]{1,0:T(8,128)} %get-tuple-element.78, f32[16384]{0:T(1024)S(1)} %all_gather.14), kind=kLoop, calls=%fused_computation.16 | loop fusion | flops 50330624 | bytes 67178496 | tf_op jit(solution)/shard_map/reduce_max | solution.py:42
  451.5 19.1 %pmax.23 = f32[1024]{0:T(1024)S(1)} all-reduce(f32[1024]{0:T(1024)S(1)} %subtract_reduce_fusion.1), channel_id=1, replica_groups=mesh['samp'=8,'state'=4] {'samp'}, use_global_device_ids=true, to_apply=%region_21.0 | all-reduce | flops 1024 | bytes 8192 | tf_op jit(solution)/shard_map/pmax | solution.py:42
  470.7 21.4 %exponential_reduce_fusion.1 = f32[1024]{0:T(1024)S(1)} fusion(f32[1024,16384]{1,0:T(8,128)} %get-tuple-element.78, f32[1024]{0:T(1024)S(1)} %pmax.23, f32[16384]{0:T(1024)S(1)} %all_gather.14), kind=kLoop, calls=%fused_computation.9 | loop fusion | flops 67107840 | bytes 67182592 | tf_op jit(solution)/shard_map/reduce_sum | solution.py:43
  492.1 17.1 %psum.37 = f32[1024]{0:T(1024)S(1)} all-reduce(f32[1024]{0:T(1024)S(1)} %exponential_reduce_fusion.1), channel_id=1, replica_groups=mesh['samp'=8,'state'=4] {'samp'}, use_global_device_ids=true, to_apply=%region_23.0 | all-reduce | flops 1024 | bytes 8192 | tf_op jit(solution)/shard_map/psum | solution.py:43
  509.2 21.5 %subtract_reduce_fusion = f32[16384]{0:T(1024)} fusion(f32[1024,16384]{1,0:T(8,128)} %get-tuple-element.78, f32[1024]{0:T(1024)S(1)} %get-tuple-element.126), kind=kLoop, calls=%fused_computation.15 | loop fusion | flops 33538048 | bytes 67178496 | tf_op jit(solution)/shard_map/reduce_max | solution.py:24
  534.1 167.1 %while.11 = (s32[]{:T(128)}, f32[32,512]{1,0:T(8,128)S(1)}, s32[32]{0:T(128)S(1)}, s32[16384]{0:T(1024)S(1)}, f32[1024]{0:T(1024)S(1)}, /*index=5*/bf16[1024,163...) while((s32[]{:T(128)}, f32[32,512]{1,0:T(8,128)S(1)}, ...), condition=%wide.region_27.0_spmd.clone, body=%wide.region_25.27_spmd.clone.sunk | while | flops 3145226 | bytes 5308661 | solution.py:71
  701.2 24.3 %exponential_reduce_fusion = f32[16384]{0:T(1024)} fusion(f32[1024,16384]{1,0:T(8,128)} %get-tuple-element.78, f32[16384]{0:T(1024)} %subtract_reduce_fusion, f32[1024]{0:T(1024)S(1)} %get-tuple-element.166), kind=kLoop, calls=%fused_computation.8 | loop fusion | flops 50315264 | bytes 67244032 | tf_op jit(solution)/shard_map/reduce_sum | solution.py:25
  727.3 8.5 %psum.38 = f32[]{:T(128)} all-reduce(f32[]{:T(128)} %bitcast.7), channel_id=1, replica_groups=mesh['samp'=8,'state'=4] {'state'}, use_global_device_ids=true, to_apply=%region_24.0 | all-reduce | flops 1 | bytes 8 | tf_op jit(solution)/shard_map/psum | solution.py:11
  748.5 8.5 %all-reduce.2.cloned.1.call-done = f32[16384]{0:T(1024)} async-done(((f32[16384]{0:T(1024)}), f32[16384]{0:T(1024)}) %all-reduce.2.cloned.1.call-update) | async-done | bytes 65552 | tf_op jit(solution)/shard_map/psum | solution.py:85
  (243 shorter events, 193.2 us)
Async XLA Ops:
  104.5 28.7 %all-to-all-start = ((f32[4,1,4096]{2,1,0:T(1,128)}), f32[4,1,4096]{2,1,0:T(1,128)S(1)}, u32[]{:S(2)}, u32[]{:S(2)}) async-start(f32[4,1,4096]{2,1,0:T(1,128)} %bitcast), calls=%async_computation | async-start | bytes 131072 | tf_op jit(solution)/shard_map/all_to_all | solution.py:28
  133.2 7.4 all-to-all-start.1
  146.0 81.7 %copy-start.2 = (s32[1024]{0:T(1024)S(1)}, s32[1024]{0:T(1024)}, u32[]{:S(2)}) copy-start(s32[1024]{0:T(1024)} %param.8) | copy-start | bytes 12292
  249.2 27.7 %all-to-all-start.2 = ((f32[4,1,4096]{2,1,0:T(1,128)}), f32[4,1,4096]{2,1,0:T(1,128)S(1)}, u32[]{:S(2)}, u32[]{:S(2)}) async-start(f32[4,1,4096]{2,1,0:T(1,128)} %bitcast.2), calls=%async_computation.2 | async-start | bytes 131072 | tf_op jit(solution)/shard_map/all_to_all | solution.py:28
  276.9 7.4 all-to-all-start.3
  368.5 52.6 %copy-start.1 = (s32[16384]{0:T(1024)S(1)}, s32[16384]{0:T(1024)}, u32[]{:S(2)}) copy-start(s32[16384]{0:T(1024)} %param.9) | copy-start | bytes 196612
  390.0 27.7 %all-to-all-start.4 = ((f32[4,1,4096]{2,1,0:T(1,128)}), f32[4,1,4096]{2,1,0:T(1,128)S(1)}, u32[]{:S(2)}, u32[]{:S(2)}) async-start(f32[4,1,4096]{2,1,0:T(1,128)} %bitcast.4), calls=%async_computation.4 | async-start | bytes 131072 | tf_op jit(solution)/shard_map/all_to_all | solution.py:28
  417.8 7.4 all-to-all-start.5
  470.7 63.4 %copy-start = (f32[1024,128]{1,0:T(8,128)S(1)}, f32[1024,128]{1,0:T(8,128)}, u32[]{:S(2)}) copy-start(f32[1024,128]{1,0:T(8,128)} %param.7) | copy-start | bytes 1572868
  530.7 205.0 %all-to-all-start.6 = ((f32[4,1,4096]{2,1,0:T(1,128)}), f32[4,1,4096]{2,1,0:T(1,128)S(1)}, u32[]{:S(2)}, u32[]{:S(2)}) async-start(f32[4,1,4096]{2,1,0:T(1,128)} %bitcast.8), calls=%async_computation.6 | async-start | bytes 131072 | tf_op jit(solution)/shard_map/all_to_all | solution.py:28
  534.0 223.0 %all-reduce.2.cloned.1.call-start = ((), (), s32[]{:S(2)}) async-start(), calls=%async_computation.8 | async-start | bytes 131072 | tf_op jit(solution)/shard_map/psum | solution.py:85
  735.8 7.4 all-to-all-start.7
Sparse Core Ops, SparseCore 0:
  726.3 30.6 all-reduce.1
where the time goes:
time: 768 us; the launch traced here: 765 us
  other arithmetic  423 us (55%)
  blocking collectives  141 us (18%)
  local copies, waits for them, and re-layouts  93.4 us (12%)
  loops' own time  42.3 us (6%)
  starting transfers between devices  27.3 us (4%)
  waiting for transfers between devices  23.3 us (3%)
  between operations  14.9 us (2%)
    reduce_max x4, other arithmetic, sample_denominator(): best = jnp.max(terms, axis=0)  139 us
    reduce_sum x4, other arithmetic, sample_denominator(): total = jnp.sum(jnp.exp(terms - best[None, :]), axis=0)  97.6 us
    reduce_sum x3, other arithmetic, state_update(): total = lax.psum(jnp.sum(jnp.exp(terms - best[:, None]), axis=1), 'samp')  64.2 us
    reduce_max x3, other arithmetic, state_update(): best = lax.pmax(jnp.max(terms, axis=1), 'samp')  63 us
    pmax x3, blocking collectives, state_update(): best = lax.pmax(jnp.max(terms, axis=1), 'samp')  60.6 us
    reduce_sum x32, other arithmetic, one(): return jnp.sum(jnp.where(match, lead[:, None] - energy_part, 0.0), axis=0)  54.7 us
    psum x3, blocking collectives, state_update(): total = lax.psum(jnp.sum(jnp.exp(terms - best[:, None]), axis=1), 'samp')  51.4 us
    another operation x1, loops' own time, own_terms_local(): return lax.map(one, jnp.arange(steps_count, dtype=jnp.int32)).reshape(width)  42.3 us
  transfers between devices with their start and end apart: 9, of which 5 were waited for; matrix products, arithmetic and copies ran while one was open for 29% of the time, Pallas kernels for 0%

commit v1 on v0

v1 whole, which is shorter than its diff:
```python
import functools

import jax
import jax.numpy as jnp
from jax import lax
from jax.experimental import pallas as pl
from jax.experimental.pallas import tpu as pltpu
from jax.sharding import PartitionSpec as P

ITERS = 3
SUB = 8
LANE = 128
NT = (((1,), (1,)), ((), ()))


def kernel(ns, np_, nc, eng, off, cnt, lab, free_o, own_o, E, offT, pick, dbuf, obuf, fbuf, abuf, lead_s, m_s, s_s,
           load_sem, dss, drs, oss, ors, fss, frs, ass, ars):
    rows = E.shape[1]
    gw = E.shape[2]
    groups = E.shape[0]
    per = groups // nc
    st = lax.axis_index("state")
    sp = lax.axis_index("samp")

    def load(g):
        return pltpu.make_async_copy(eng.at[:, pl.ds(pl.multiple_of(g * gw, gw), gw)], E.at[g], load_sem.at[g])

    @pl.loop(0, groups)
    def _(g):
        load(g).start()

    barrier = pltpu.get_barrier_semaphore()
    for s in range(1, ns):
        pl.semaphore_signal(barrier, inc=1, device_id={"state": lax.rem(st + s, ns)})
    for s in range(1, np_):
        pl.semaphore_signal(barrier, inc=1, device_id={"samp": lax.rem(sp + s, np_)})

    offT[...] = off[...].T.reshape(groups, SUB, rows)
    logc = jnp.log(cnt[...].astype(jnp.float32))
    lead_s[...] = logc
    pl.semaphore_wait(barrier, ns + np_ - 2)

    rowid = lax.broadcasted_iota(jnp.int32, (SUB, LANE), 0)

    def split(x):
        hi = x.astype(jnp.bfloat16)
        lo = (x - hi.astype(jnp.float32)).astype(jnp.bfloat16)
        return jnp.concatenate([hi, lo], axis=0)

    def dcopy(it, c, s):
        part = dbuf.at[it, st, pl.ds(c * per, per)]
        return pltpu.make_async_remote_copy(
            part, part, dss.at[it, c, s - 1], drs.at[it, c, s - 1], device_id={"state": lax.rem(st + s, ns)})

    def ocopy(c, s):
        part = obuf.at[st, pl.ds(c * per, per)]
        return pltpu.make_async_remote_copy(
            part, part, oss.at[c, s - 1], ors.at[c, s - 1], device_id={"state": lax.rem(st + s, ns)})

    def denom_group(it, g, last):
        a = lead_s[...] - offT[g]
        top = jnp.max(a, axis=1, keepdims=True)
        w = split(jnp.exp(a - top))
        out = jnp.dot(w, E[g], preferred_element_type=jnp.float32)
        out = out[:SUB] + out[SUB:]
        tot = out[:, :LANE]
        for i in range(1, SUB):
            tot = jnp.where(rowid == i, out[:, i * LANE:(i + 1) * LANE], tot)
        dbuf[it, st, g] = top + jnp.log(tot)
        if last:
            label = lab[g] - st * rows
            low = label & (LANE - 1)
            high = label >> 7
            sel = jnp.zeros((SUB, LANE), jnp.float32)
            for h in range(rows // LANE):
                got = jnp.take_along_axis(a[:, h * LANE:(h + 1) * LANE], low, axis=1)
                sel = jnp.where(high == h, got, sel)
            obuf[st, g] = sel - pick[g]

    def exp_group(g):
        load(g).wait()
        for i in range(SUB):
            label = jnp.broadcast_to(lab[g, i:i + 1, :] - st * rows, (16, LANE))
            ids = lax.broadcasted_iota(jnp.int32, (16, LANE), 0)

            def body(k, acc):
                for q in range(8):
                    r0 = pl.multiple_of(k * 128 + q * 16, 16)
                    e = E[g, pl.ds(r0, 16), i * LANE:(i + 1) * LANE].astype(jnp.float32)
                    E[g, pl.ds(r0, 16), i * LANE:(i + 1) * LANE] = jnp.exp(-e).astype(jnp.bfloat16)
                    acc = jnp.where(label - r0 == ids, e, acc)
                return acc

            acc = lax.fori_loop(0, rows // 128, body, jnp.zeros((16, LANE), jnp.float32))
            pick[g, i:i + 1, :] = jnp.sum(acc, axis=0, keepdims=True)

    def denominator(it, last):
        @pl.loop(0, nc)
        def _(c):
            @pl.loop(0, per)
            def _(j):
                g = c * per + j
                if it == 0:
                    exp_group(g)
                denom_group(it, g, last)
            for s in range(1, ns):
                dcopy(it, c, s).start()
                if last:
                    ocopy(c, s).start()

    def join(it, g):
        vals = [dbuf[it, q, g] for q in range(ns)]
        top = functools.reduce(jnp.maximum, vals)
        return top + jnp.log(sum(jnp.exp(v - top) for v in vals))

    def fcopy(it, s):
        return pltpu.make_async_remote_copy(
            fbuf.at[it, sp], fbuf.at[it, sp], fss.at[it, s - 1], frs.at[it, s - 1],
            device_id={"samp": lax.rem(sp + s, np_)})

    def update(it):
        m_s[...] = jnp.full(m_s.shape, -1e30, jnp.float32)
        s_s[...] = jnp.zeros(s_s.shape, jnp.float32)

        @pl.loop(0, nc)
        def _(c):
            for s in range(1, ns):
                dcopy(it, c, s).wait()

            @pl.loop(0, per)
            def _(j):
                g = c * per + j
                d = join(it, g)
                low = jnp.min(d, axis=1, keepdims=True)
                r = jnp.exp(low - d)
                spread = jnp.concatenate([jnp.where(rowid == i, r, 0.0) for i in range(SUB)], axis=1)
                out = lax.dot_general(split(spread), E[g], NT, preferred_element_type=jnp.float32)
                x = jnp.log(out[:SUB] + out[SUB:]) - offT[g] - low
                m = m_s[...]
                new = jnp.maximum(m, x)
                s_s[...] = s_s[...] * jnp.exp(m - new) + jnp.exp(x - new)
                m_s[...] = new

        m = m_s[...]
        top = jnp.max(m, axis=0, keepdims=True)
        fbuf[it, sp] = top + jnp.log(jnp.sum(s_s[...] * jnp.exp(m - top), axis=0, keepdims=True))
        for s in range(1, np_):
            fcopy(it, s).start()
        for s in range(1, np_):
            fcopy(it, s).wait()
        vals = [fbuf[it, q] for q in range(np_)]
        top = functools.reduce(jnp.maximum, vals)
        return -(top + jnp.log(sum(jnp.exp(v - top) for v in vals)))

    free = None
    denominator(0, False)
    for it in range(ITERS):
        free = update(it)
        lead_s[...] = logc + free
        if it < ITERS - 1:
            denominator(it + 1, False)

    def acopy(s):
        return pltpu.make_async_remote_copy(
            abuf.at[st], abuf.at[st], ass.at[s - 1], ars.at[s - 1], device_id={"state": lax.rem(st + s, ns)})

    abuf[st] = free[:, :LANE]
    for s in range(1, ns):
        acopy(s).start()
    denominator(ITERS, True)
    for s in range(1, ns):
        acopy(s).wait()
    free_o[...] = free - abuf[0][:, 0:1]

    @pl.loop(0, nc)
    def _(c):
        for s in range(1, ns):
            dcopy(ITERS, c, s).wait()
            ocopy(c, s).wait()

        @pl.loop(0, per)
        def _(j):
            g = c * per + j
            own_o[g] = sum(obuf[q, g] for q in range(ns)) - join(ITERS, g)


def solution(mesh):
    ns, np_ = mesh.shape["state"], mesh.shape["samp"]

    def shards(energies, offsets, counts, labels):
        rows, width = energies.shape
        nblk = offsets.shape[1]
        groups = nblk // SUB
        gw = width // groups
        nc = 4
        dma = pltpu.SemaphoreType.DMA
        vm = pl.BlockSpec(memory_space=pltpu.VMEM)
        free, own = pl.pallas_call(
            functools.partial(kernel, ns, np_, nc),
            out_shape=(
                jax.ShapeDtypeStruct((1, rows), jnp.float32),
                jax.ShapeDtypeStruct((groups, SUB, LANE), jnp.float32),
            ),
            in_specs=[pl.BlockSpec(memory_space=pl.ANY), vm, vm, vm],
            out_specs=(vm, vm),
            scratch_shapes=[
                pltpu.VMEM((groups, rows, gw), jnp.bfloat16),
                pltpu.VMEM((groups, SUB, rows), jnp.float32),
                pltpu.VMEM((groups, SUB, LANE), jnp.float32),
                pltpu.VMEM((ITERS + 1, ns, groups, SUB, LANE), jnp.float32),
                pltpu.VMEM((ns, groups, SUB, LANE), jnp.float32),
                pltpu.VMEM((ITERS, np_, 1, rows), jnp.float32),
                pltpu.VMEM((ns, 1, LANE), jnp.float32),
                pltpu.VMEM((1, rows), jnp.float32),
                pltpu.VMEM((SUB, rows), jnp.float32),
                pltpu.VMEM((SUB, rows), jnp.float32),
                dma((groups,)),
                dma((ITERS + 1, nc, ns - 1)), dma((ITERS + 1, nc, ns - 1)),
                dma((nc, ns - 1)), dma((nc, ns - 1)),
                dma((ITERS, np_ - 1)), dma((ITERS, np_ - 1)),
                dma((ns - 1,)), dma((ns - 1,)),
            ],
            compiler_params=pltpu.CompilerParams(
                collective_id=0, has_side_effects=True, vmem_limit_bytes=60 * 1024 * 1024),
            name="mbar",
        )(energies, offsets, counts.reshape(1, rows), labels.reshape(groups, SUB, LANE))
        return free.reshape(rows), own.reshape(width)

    return jax.shard_map(
        shards,
        mesh=mesh,
        in_specs=(P("state", "samp"), P("state", "samp"), P("state"), P("samp")),
        out_specs=(P("state"), P("samp")),
        check_vma=False,
    )
```

time: 768 us -> 201 us (0.26)
  other arithmetic: 423 us -> 0 us
  Pallas kernels: 0 us -> 198 us
  blocking collectives: 141 us -> 0 us
  local copies, waits for them, and re-layouts: 93.4 us -> 2.74 us
  loops' own time: 42.3 us -> 0 us
  starting transfers between devices: 27.3 us -> 0 us
  waiting for transfers between devices: 23.3 us -> 0 us
  between operations: 14.9 us -> 0.64 us
    reduce_sum x43 -> x0, other arithmetic: 217 us -> none  [the longest x4 97.6 us: sample_denominator(): total = jnp.sum(jnp.exp(terms - best[None, :]), axis=0)]
    reduce_max x11 -> x0, other arithmetic: 202 us -> none  [the longest x4 139 us: sample_denominator(): best = jnp.max(terms, axis=0)]
    pallas_call x0 -> x1, Pallas kernels: none -> 198 us  [shards(): pl.pallas_call(functools.partial(kernel, ns, np_, nc), out_shape=(jax.Sha...]
    add x33 -> x0, local copies, waits for them, and re-layouts: 61.6 us -> none  [the longest x32 39.4 us: one(): part.reshape(rows, span // block_size, block_size) + shift[:, :, None]]
    pmax x3 -> x0, blocking collectives: 60.6 us -> none  [state_update(): best = lax.pmax(jnp.max(terms, axis=1), 'samp')]
    psum x4 -> x0, blocking collectives: 59.9 us -> none  [the longest x3 51.4 us: state_update(): total = lax.psum(jnp.sum(jnp.exp(terms - best[:, None]), axis=1), 'samp')]
    another operation x1 -> x0, loops' own time: 42.3 us -> none  [own_terms_local(): return lax.map(one, jnp.arange(steps_count, dtype=jnp.int32)).reshape(width)]
    dynamic_slice x96 -> x0, local copies, waits for them, and re-layouts: 28.6 us -> none  [the longest x32 19.6 us: own_terms_local(): return lax.map(one, jnp.arange(steps_count, dtype=jnp.int32)).reshape(width)]
  transfers between devices with their start and end apart: 9 -> 0, of which waited for: 5 -> 0; matrix products, arithmetic and copies ran while one was open for 29% -> 0% of each run, Pallas kernels for 0% -> 0%
where the time goes in v1:
time: 201 us
  Pallas kernels  198 us (99%)
  local copies, waits for them, and re-layouts  2.74 us (1%)
    pallas_call x1, Pallas kernels, shards(): pl.pallas_call(functools.partial(kernel, ns, np_, nc), out_shape=(jax.Sha...  198 us

profile of v1, /device:TPU:0, one launch (start us, length us, event | category | flops | bytes accessed | tf_op | source)
XLA Modules:
  0.0 201.0 jit_solution(2134200072903463103)
XLA Ops:
  0.6 197.6 %mbar.1 = (f32[1,1024]{1,0:T(1,128)}, f32[16,8,128]{2,1,0:T(8,128)}) custom-call(bf16[1024,16384]{1,0:T(8,128)(2,1)} %eng.1, f32[1024,128]{1,0:T(8,128)} %off.1, s32[1,1024]{1,0:T(1,128)} %bitcast.6, s32[16,8,128]{2,1,0:T(8,128)} %bitcast.4), custom_call_target="tpu_custom_call" | custom-call | tf_op jit(solution)/shard_map/mbar/pallas_call | solution.py:198
  198.3 1.3 copy.8
  199.5 1.5 copy.9

commit v2 on v1

--- a/solution.py
+++ b/solution.py
@@ -10,6 +10,7 @@
 ITERS = 3
 SUB = 8
 LANE = 128
+NLOG2E = -1.4426950408889634
 NT = (((1,), (1,)), ((), ()))
 
 
@@ -57,15 +58,22 @@
         return pltpu.make_async_remote_copy(
             part, part, oss.at[c, s - 1], ors.at[c, s - 1], device_id={"state": lax.rem(st + s, ns)})
 
-    def denom_group(it, g, last):
+    def weights(g):
         a = lead_s[...] - offT[g]
         top = jnp.max(a, axis=1, keepdims=True)
-        w = split(jnp.exp(a - top))
-        out = jnp.dot(w, E[g], preferred_element_type=jnp.float32)
+        return a, top, split(jnp.exp(a - top))
+
+    def place(tot, c, out):
         out = out[:SUB] + out[SUB:]
-        tot = out[:, :LANE]
-        for i in range(1, SUB):
-            tot = jnp.where(rowid == i, out[:, i * LANE:(i + 1) * LANE], tot)
+        tot = jnp.where(rowid == 2 * c, out[:, :LANE], tot)
+        return jnp.where(rowid == 2 * c + 1, out[:, LANE:], tot)
+
+    def denom_group(it, g, last):
+        a, top, w = weights(g)
+        tot = jnp.zeros((SUB, LANE), jnp.float32)
+        for c in range(SUB // 2):
+            out = jnp.dot(w, E[g, :, 2 * c * LANE:2 * (c + 1) * LANE], preferred_element_type=jnp.float32)
+            tot = place(tot, c, out)
         dbuf[it, st, g] = top + jnp.log(tot)
         if last:
             label = lab[g] - st * rows
@@ -77,22 +85,38 @@
                 sel = jnp.where(high == h, got, sel)
             obuf[st, g] = sel - pick[g]
 
-    def exp_group(g):
+    def first_group(g):
         load(g).wait()
-        for i in range(SUB):
-            label = jnp.broadcast_to(lab[g, i:i + 1, :] - st * rows, (16, LANE))
-            ids = lax.broadcasted_iota(jnp.int32, (16, LANE), 0)
-
-            def body(k, acc):
-                for q in range(8):
-                    r0 = pl.multiple_of(k * 128 + q * 16, 16)
-                    e = E[g, pl.ds(r0, 16), i * LANE:(i + 1) * LANE].astype(jnp.float32)
-                    E[g, pl.ds(r0, 16), i * LANE:(i + 1) * LANE] = jnp.exp(-e).astype(jnp.bfloat16)
-                    acc = jnp.where(label - r0 == ids, e, acc)
-                return acc
-
-            acc = lax.fori_loop(0, rows // 128, body, jnp.zeros((16, LANE), jnp.float32))
-            pick[g, i:i + 1, :] = jnp.sum(acc, axis=0, keepdims=True)
+        _, top, w = weights(g)
+        tot = jnp.zeros((SUB, LANE), jnp.float32)
+        ids = lax.broadcasted_iota(jnp.int32, (16, LANE), 0)
+        for c in range(SUB // 2):
+            high, low, acc = [], [], []
+            for h in range(2):
+                label = jnp.broadcast_to(lab[g, 2 * c + h:2 * c + h + 1, :] - st * rows, (16, LANE))
+                high.append((label >> 4).astype(jnp.int16))
+                low.append(label & 15)
+                acc.append(jnp.zeros((16, LANE), jnp.bfloat16))
+            out = jnp.zeros((2 * SUB, 2 * LANE), jnp.float32)
+            for k in range(rows // 512):
+                tiles = []
+                for q in range(k * 32, (k + 1) * 32):
+                    pair = []
+                    for h in range(2):
+                        at = (g, slice(q * 16, (q + 1) * 16), slice((2 * c + h) * LANE, (2 * c + h + 1) * LANE))
+                        e = E[at]
+                        v = jnp.exp2(e.astype(jnp.float32) * NLOG2E).astype(jnp.bfloat16)
+                        E[at] = v
+                        pair.append(v)
+                        acc[h] = jnp.where(high[h] == jnp.int16(q), e, acc[h])
+                    tiles.append(jnp.concatenate(pair, axis=1))
+                out += jnp.dot(w[:, k * 512:(k + 1) * 512], jnp.concatenate(tiles, axis=0),
+                               preferred_element_type=jnp.float32)
+            for h in range(2):
+                got = jnp.where(low[h] == ids, acc[h].astype(jnp.float32), 0.0)
+                pick[g, 2 * c + h:2 * c + h + 1, :] = jnp.sum(got, axis=0, keepdims=True)
+            tot = place(tot, c, out)
+        dbuf[0, st, g] = top + jnp.log(tot)
 
     def denominator(it, last):
         @pl.loop(0, nc)
@@ -101,8 +125,9 @@
             def _(j):
                 g = c * per + j
                 if it == 0:
-                    exp_group(g)
-                denom_group(it, g, last)
+                    first_group(g)
+                else:
+                    denom_group(it, g, last)
             for s in range(1, ns):
                 dcopy(it, c, s).start()
                 if last:
@@ -134,12 +159,15 @@
                 low = jnp.min(d, axis=1, keepdims=True)
                 r = jnp.exp(low - d)
                 spread = jnp.concatenate([jnp.where(rowid == i, r, 0.0) for i in range(SUB)], axis=1)
-                out = lax.dot_general(split(spread), E[g], NT, preferred_element_type=jnp.float32)
-                x = jnp.log(out[:SUB] + out[SUB:]) - offT[g] - low
-                m = m_s[...]
-                new = jnp.maximum(m, x)
-                s_s[...] = s_s[...] * jnp.exp(m - new) + jnp.exp(x - new)
-                m_s[...] = new
+                lhs = split(spread)
+                for q in range(rows // 256):
+                    sl = slice(q * 256, (q + 1) * 256)
+                    out = lax.dot_general(lhs, E[g, sl, :], NT, preferred_element_type=jnp.float32)
+                    x = jnp.log(out[:SUB] + out[SUB:]) - offT[g, :, sl] - low
+                    m = m_s[:, sl]
+                    new = jnp.maximum(m, x)
+                    s_s[:, sl] = s_s[:, sl] * jnp.exp(m - new) + jnp.exp(x - new)
+                    m_s[:, sl] = new
 
         m = m_s[...]
         top = jnp.max(m, axis=0, keepdims=True)

time: 201 us -> 101 us (0.50)
  Pallas kernels: 198 us -> 97.3 us
    pallas_call x1, Pallas kernels: 198 us -> 97.3 us  [shards(): pl.pallas_call(functools.partial(kernel, ns, np_, nc), out_shape=(jax.Sha...]
where the time goes in v2:
time: 101 us
  Pallas kernels  97.3 us (96%)
  local copies, waits for them, and re-layouts  2.74 us (3%)
    pallas_call x1, Pallas kernels, shards(): pl.pallas_call(functools.partial(kernel, ns, np_, nc), out_shape=(jax.Sha...  97.3 us
    unnamed x2, local copies, waits for them, and re-layouts  2.74 us

profile of v2, /device:TPU:0, one launch (start us, length us, event | category | flops | bytes accessed | tf_op | source)
XLA Modules:
  0.0 100.7 jit_solution(11456958491476536763)
XLA Ops:
  0.6 97.3 %mbar.1 = (f32[1,1024]{1,0:T(1,128)}, f32[16,8,128]{2,1,0:T(8,128)}) custom-call(bf16[1024,16384]{1,0:T(8,128)(2,1)} %eng.1, f32[1024,128]{1,0:T(8,128)} %off.1, s32[1,1024]{1,0:T(1,128)} %bitcast.6, s32[16,8,128]{2,1,0:T(8,128)} %bitcast.4), custom_call_target="tpu_custom_call" | custom-call | tf_op jit(solution)/shard_map/mbar/pallas_call | solution.py:226
  97.9 1.3 %copy.8 = f32[1024]{0:T(1024)} copy(f32[1024]{0:T(1024)} %bitcast.7) | data formatting | bytes 8192
  99.2 1.5 %copy.9 = f32[16384]{0:T(1024)} copy(f32[16384]{0:T(1024)} %bitcast.5) | data formatting | bytes 131072

commit v3 on v2

--- a/solution.py
+++ b/solution.py
@@ -14,9 +14,10 @@
 NT = (((1,), (1,)), ((), ()))
 
 
-def kernel(ns, np_, nc, eng, off, cnt, lab, free_o, own_o, E, offT, pick, dbuf, obuf, fbuf, abuf, lead_s, m_s, s_s,
+def kernel(ns, np_, nc, eng, off, cnt, lab, free_o, own_o, E, offT, pick, dbuf, obuf, fbuf, abuf, lead_s, m_s, s_s, T, low_s,
            load_sem, dss, drs, oss, ors, fss, frs, ass, ars):
     rows = E.shape[1]
+    nm, nv = m_s.shape[1], rows - m_s.shape[1]
     gw = E.shape[2]
     groups = E.shape[0]
     per = groups // nc
@@ -39,6 +40,7 @@
     offT[...] = off[...].T.reshape(groups, SUB, rows)
     logc = jnp.log(cnt[...].astype(jnp.float32))
     lead_s[...] = logc
+    T[...] = jnp.zeros(T.shape, jnp.float32)
     pl.semaphore_wait(barrier, ns + np_ - 2)
 
     rowid = lax.broadcasted_iota(jnp.int32, (SUB, LANE), 0)
@@ -121,13 +123,13 @@
     def denominator(it, last):
         @pl.loop(0, nc)
         def _(c):
-            @pl.loop(0, per)
-            def _(j):
-                g = c * per + j
-                if it == 0:
-                    first_group(g)
-                else:
-                    denom_group(it, g, last)
+            if it == 0:
+                @pl.loop(0, per)
+                def _(j):
+                    first_group(c * per + j)
+            else:
+                for j in range(per):
+                    denom_group(it, c * per + j, last)
             for s in range(1, ns):
                 dcopy(it, c, s).start()
                 if last:
@@ -143,6 +145,29 @@
             fbuf.at[it, sp], fbuf.at[it, sp], fss.at[it, s - 1], frs.at[it, s - 1],
             device_id={"samp": lax.rem(sp + s, np_)})
 
+    def update_group(it, g):
+        d = join(it, g)
+        low = jnp.min(d, axis=1, keepdims=True)
+        r = jnp.exp(low - d)
+        low_s[g] = jnp.broadcast_to(low, (SUB, LANE))
+        lhs = split(jnp.concatenate([jnp.where(rowid == i, r, 0.0) for i in range(SUB)], axis=1))
+        for q in range(0, nm, 256):
+            sl = slice(q, min(nm, q + 256))
+            out = lax.dot_general(lhs, E[g, sl, :], NT, preferred_element_type=jnp.float32)
+            x = jnp.log(out[:SUB] + out[SUB:]) - offT[g, :, sl] - low
+            m = m_s[:, sl]
+            new = jnp.maximum(m, x)
+            s_s[:, sl] = s_s[:, sl] * jnp.exp(m - new) + jnp.exp(x - new)
+            m_s[:, sl] = new
+        wide = [jnp.broadcast_to(r[i:i + 1, :], (16, LANE)) for i in range(SUB)]
+        lane = lax.broadcasted_iota(jnp.int32, (16, LANE), 1)
+        for t in range(0, nv, 16):
+            acc = T[t:t + 16, :]
+            for i in range(SUB):
+                v = E[g, nm + t:nm + t + 16, i * LANE:(i + 1) * LANE].astype(jnp.float32) * wide[i]
+                acc = jnp.where(lane == g * SUB + i, jnp.sum(v, axis=1, keepdims=True), acc)
+            T[t:t + 16, :] = acc
+
     def update(it):
         m_s[...] = jnp.full(m_s.shape, -1e30, jnp.float32)
         s_s[...] = jnp.zeros(s_s.shape, jnp.float32)
@@ -152,26 +177,16 @@
             for s in range(1, ns):
                 dcopy(it, c, s).wait()
 
-            @pl.loop(0, per)
-            def _(j):
-                g = c * per + j
-                d = join(it, g)
-                low = jnp.min(d, axis=1, keepdims=True)
-                r = jnp.exp(low - d)
-                spread = jnp.concatenate([jnp.where(rowid == i, r, 0.0) for i in range(SUB)], axis=1)
-                lhs = split(spread)
-                for q in range(rows // 256):
-                    sl = slice(q * 256, (q + 1) * 256)
-                    out = lax.dot_general(lhs, E[g, sl, :], NT, preferred_element_type=jnp.float32)
-                    x = jnp.log(out[:SUB] + out[SUB:]) - offT[g, :, sl] - low
-                    m = m_s[:, sl]
-                    new = jnp.maximum(m, x)
-                    s_s[:, sl] = s_s[:, sl] * jnp.exp(m - new) + jnp.exp(x - new)
-                    m_s[:, sl] = new
+            for j in range(per):
+                update_group(it, c * per + j)
 
         m = m_s[...]
         top = jnp.max(m, axis=0, keepdims=True)
-        fbuf[it, sp] = top + jnp.log(jnp.sum(s_s[...] * jnp.exp(m - top), axis=0, keepdims=True))
+        fbuf[it, sp, :, 0:nm] = top + jnp.log(jnp.sum(s_s[...] * jnp.exp(m - top), axis=0, keepdims=True))
+        if nv:
+            x = jnp.log(T[...].T).reshape(groups, SUB, nv) - offT[:, :, nm:] - low_s[:, :, 0:1]
+            top = jnp.max(x, axis=(0, 1), keepdims=True)
+            fbuf[it, sp, :, nm:] = (top + jnp.log(jnp.sum(jnp.exp(x - top), axis=(0, 1), keepdims=True)))[0]
         for s in range(1, np_):
             fcopy(it, s).start()
         for s in range(1, np_):
@@ -221,6 +236,7 @@
         groups = nblk // SUB
         gw = width // groups
         nc = 4
+        nv = rows // 4 if nblk == LANE else 0
         dma = pltpu.SemaphoreType.DMA
         vm = pl.BlockSpec(memory_space=pltpu.VMEM)
         free, own = pl.pallas_call(
@@ -240,8 +256,10 @@
                 pltpu.VMEM((ITERS, np_, 1, rows), jnp.float32),
                 pltpu.VMEM((ns, 1, LANE), jnp.float32),
                 pltpu.VMEM((1, rows), jnp.float32),
-                pltpu.VMEM((SUB, rows), jnp.float32),
-                pltpu.VMEM((SUB, rows), jnp.float32),
+                pltpu.VMEM((SUB, rows - nv), jnp.float32),
+                pltpu.VMEM((SUB, rows - nv), jnp.float32),
+                pltpu.VMEM((max(nv, 16), LANE), jnp.float32),
+                pltpu.VMEM((groups, SUB, LANE), jnp.float32),
                 dma((groups,)),
                 dma((ITERS + 1, nc, ns - 1)), dma((ITERS + 1, nc, ns - 1)),
                 dma((nc, ns - 1)), dma((nc, ns - 1)),

time: 101 us -> 81.4 us (0.81)
  Pallas kernels: 97.3 us -> 77.8 us
    pallas_call x1, Pallas kernels: 97.3 us -> 77.8 us  [shards(): pl.pallas_call(functools.partial(kernel, ns, np_, nc), out_shape=(jax.Sha...]
where the time goes in v3:
time: 81.4 us; the launch traced here: 81.2 us
  Pallas kernels  77.8 us (96%)
  local copies, waits for them, and re-layouts  2.74 us (3%)
    pallas_call x1, Pallas kernels, shards(): pl.pallas_call(functools.partial(kernel, ns, np_, nc), out_shape=(jax.Sha...  77.8 us
    unnamed x2, local copies, waits for them, and re-layouts  2.74 us

profile of v3, /device:TPU:0, one launch (start us, length us, event | category | flops | bytes accessed | tf_op | source)
XLA Modules:
  0.0 81.2 jit_solution(6383980310936114592)
XLA Ops:
  0.6 77.8 %mbar.1 = (f32[1,1024]{1,0:T(1,128)}, f32[16,8,128]{2,1,0:T(8,128)}) custom-call(bf16[1024,16384]{1,0:T(8,128)(2,1)} %eng.1, f32[1024,128]{1,0:T(8,128)} %off.1, s32[1,1024]{1,0:T(1,128)} %bitcast.6, s32[16,8,128]{2,1,0:T(8,128)} %bitcast.4), custom_call_target="tpu_custom_call" | custom-call | tf_op jit(solution)/shard_map/mbar/pallas_call | solution.py:242
  78.5 1.3 %copy.8 = f32[1024]{0:T(1024)} copy(f32[1024]{0:T(1024)} %bitcast.7) | data formatting | bytes 8192
  79.7 1.5 %copy.9 = f32[16384]{0:T(1024)} copy(f32[16384]{0:T(1024)} %bitcast.5) | data formatting | bytes 131072
